TPU v7x, 256 devices: a whole 4x4x8 slice. The times are simulated.
256 devices in a mesh: seq: 8 (over y, core), vocab: 32 (over z, x).
Axes of the slice: x: 4, y: 4, z: 8, core: 2. Of those that a mesh axis runs over, the one named last changes fastest.
Arguments:
- hidden: bfloat16 [2, 1024, 5120], P(None, 'seq'), may hold values from -128 to 128
- head_weight: bfloat16 [5120, 77824], P('seq', 'vocab'), may hold values from -1 to 1
- ref_logits: bfloat16 [2, 1024, 77824], P(None, 'seq', 'vocab'), may hold values from -320 to 320
- token_ids: int32 [2, 1024], P(None, 'seq'), may hold values from 0 to 77823
- end_pos: int32 [2], replicated, may hold values from 512 to 1023
- loss_mask: int32 [2, 1024], P(None, 'seq'), may hold values 0 or 1
- scores: float32 [2], replicated, may hold values from -8 to 8
Outputs:
- logit_grad: bfloat16 [2, 1024, 77824], P(None, 'seq', 'vocab')
- hidden_grad: bfloat16 [2, 1024, 5120], P(None, 'seq', 'vocab')
- advantages: float32 [2, 1024], P(None, 'seq')
All inputs are finite; a program needn't handle non-finite values. No bound on the sum of `loss_mask` on one device may be relied on, other than what follows from the above.
Results may differ from a plain program's by a relative error of at most 0.0039.
The roundings to bfloat16 on the way count: a program that leaves them out, or rounds other values in their place, can miss the bound.
Values may be sent and summed in bfloat16 or wider, within the bound.
No kernel may reach another device: no remote copies, remote signals or barrier semaphores. Data moves between devices by JAX's collectives and lax.ppermute only.
A program may use at most 128 MiB of HBM per device.

v0:
```python
import jax
import jax.numpy as jnp
from jax import lax
from jax.sharding import PartitionSpec as P


def from_behind(shard, axis, by):
    devices = lax.axis_size(axis)
    pairs = [(i, i + by) for i in range(devices) if 0 <= i + by < devices]
    return lax.ppermute(shard, axis, pairs)


def per_device(hidden, head_weight, ref_logits, token_ids, end_pos, loss_mask, scores):
    batch, segment, width = hidden.shape
    vocab_dev = head_weight.shape[1]
    seq_start = lax.axis_index("seq") * segment
    vocab_start = lax.axis_index("vocab") * vocab_dev
    whole_head = lax.all_gather(head_weight, "seq", axis=0, tiled=True)
    logits = jnp.dot(
        hidden.reshape(batch * segment, width), whole_head, preferred_element_type=jnp.float32
    ).reshape(batch, segment, vocab_dev)
    refs = ref_logits.astype(jnp.float32)
    local_top = jnp.max(logits, axis=2)
    local_rtop = jnp.max(refs, axis=2)
    top_policy, top_ref = lax.pmax((local_top, local_rtop), "vocab")
    expo = jnp.exp(logits - top_policy[:, :, None])
    total, ref_total, weighted = lax.psum(
        (
            jnp.sum(expo, axis=2),
            jnp.sum(jnp.exp(refs - top_ref[:, :, None]), axis=2),
            jnp.sum(expo * (logits - refs), axis=2),
        ),
        "vocab",
    )
    lse_policy = top_policy + jnp.log(total)
    lse_ref = top_ref + jnp.log(ref_total)
    kl_value = weighted / total - lse_policy + lse_ref
    position = seq_start + lax.broadcasted_iota(jnp.int32, (1, segment), 1)
    live = ((loss_mask == 1) & (position <= end_pos[:, None])).astype(jnp.float32)
    at_end = (position == end_pos[:, None]).astype(jnp.float32)
    reward = -0.01 * kl_value * live + scores[:, None] * at_end
    upper = (
        lax.broadcasted_iota(jnp.int32, (segment, segment), 0)
        >= lax.broadcasted_iota(jnp.int32, (segment, segment), 1)
    ).astype(jnp.float32)
    local_returns = jnp.dot(reward, upper, precision=lax.Precision.HIGHEST)
    totals = jnp.sum(reward, axis=1)
    carried = jnp.zeros_like(totals)
    for _ in range(lax.axis_size("seq") - 1):
        carried = from_behind(totals + carried, "seq", -1)
    returns = local_returns + carried[:, None]
    count, first_moment, second_moment = lax.psum(
        (jnp.sum(live), jnp.sum(live * returns), jnp.sum(live * returns * returns)), "seq"
    )
    count = jnp.maximum(count, 1.0)
    mean = first_moment / count
    var = second_moment / count - mean * mean
    advantages = (returns - mean) / jnp.sqrt(var + 1e-05)
    factor = live * advantages / count
    prob = jnp.exp(logits - lse_policy[:, :, None])
    column = vocab_start + lax.broadcasted_iota(jnp.int32, (1, 1, vocab_dev), 2)
    onehot = (column == token_ids[:, :, None]).astype(jnp.float32)
    logit_grad = (factor[:, :, None] * (prob - onehot)).astype(jnp.bfloat16)
    partial_grad = lax.dot_general(
        logit_grad.reshape(batch * segment, vocab_dev),
        whole_head,
        (((1,), (1,)), ((), ())),
        preferred_element_type=jnp.float32,
    ).reshape(batch, segment, width)
    hidden_grad = lax.psum_scatter(partial_grad, "vocab", scatter_dimension=2, tiled=True).astype(
        jnp.bfloat16
    )
    return (logit_grad, hidden_grad, advantages)


def solution(mesh):
    in_specs = (
        P(None, "seq", None),
        P("seq", "vocab"),
        P(None, "seq", "vocab"),
        P(None, "seq"),
        P(),
        P(None, "seq"),
        P(),
    )
    out_specs = (P(None, "seq", "vocab"), P(None, "seq", "vocab"), P(None, "seq"))
    return jax.shard_map(
        per_device, mesh=mesh, in_specs=in_specs, out_specs=out_specs, check_vma=False
    )
```

profile of v0, /device:TPU:8, one launch (start us, length us, event | category | flops | bytes accessed | tf_op | source)
XLA Modules:
  0.0 593.1 jit_solution(15525419192187923961)
XLA Ops:
  7.2 0.0 all-gather.2.cloned.1.call-start
  7.2 0.7 all-gather.2.cloned.1.call-update
  7.9 0.0 reduce-scatter.2.cloned.1.call-start
  8.0 1.5 reduce_max.24
  9.5 124.9 %all-gather.2.cloned.1.call-done = bf16[5120,2432]{1,0:T(8,128)(2,1)} async-done(((bf16[640,2432]{1,0:T(8,128)(2,1)}), bf16[5120,2432]{1,0:T(8,128)(2,1)}) %all-gather.2.cloned.1.call-update) | async-done | bytes 24903696 | tf_op jit(solution)/shard_map/all_gather | solution.py:18
  134.5 13.4 %fusion.14 = (f32[2,128]{1,0:T(2,128)S(1)}, f32[2,128,2432]{2,1,0:T(8,128)}) fusion(bf16[2,128,5120]{2,1,0:T(8,128)(2,1)S(1)} %copy-done, bf16[5120,2432]{1,0:T(8,128)(2,1)} %all-gather.2.cloned.1.call-done), kind=kOutput, calls=%fused_computation.28 | convolution fusion | flops 6375964672 | bytes 30016512 | tf_op jit(solution)/shard_map/dot_general | solution.py:19
  147.8 75.2 %all-reduce.1 = (f32[2,128]{1,0:T(2,128)S(1)}, f32[2,128]{1,0:T(2,128)S(1)}) all-reduce(f32[2,128]{1,0:T(2,128)S(1)} %get-tuple-element.23, bf16[2,128]{1,0:T(2,128)(2,1)S(1)} %reduce_max.24), channel_id=1, replica_groups=mesh['seq'=8,'vocab'=32] {'vocab'}, use_global_device_ids=true, to_apply=%region_1.0 | all-reduce | flops 512 | bytes 3584 | tf_op jit(solution)/shard_map/pmax | solution.py:25
  223.1 3.2 fusion.5
  226.3 69.6 %all-reduce = (f32[2,128]{1,0:T(2,128)S(1)}, f32[2,128]{1,0:T(2,128)S(1)}, f32[2,128]{1,0:T(2,128)S(1)}) all-reduce(f32[2,128]{1,0:T(2,128)S(1)} %get-tuple-element.4, f32[2,128]{1,0:T(2,128)S(1)} %get-tuple-element.5, f32[2,128]{1,0:T(2,128)S(1)} %get-tuple-element.3), channel_id=1, replica_groups=mesh['seq'=8,'vocab'=32] {'vocab'}, use_global_device_ids=true, to_apply=%region_5.0 | all-reduce | flops 768 | bytes 6144 | tf_op jit(solution)/shard_map/psum | solution.py:27
  296.0 0.2 fusion.12
  296.1 1.9 collective-permute-start
  298.1 1.3 collective-permute-done
  299.4 3.6 collective-permute-start.1
  302.9 1.3 collective-permute-done.1
  304.2 3.6 collective-permute-start.2
  307.8 1.3 collective-permute-done.2
  309.1 3.6 collective-permute-start.3
  312.6 1.3 collective-permute-done.3
  313.9 3.6 collective-permute-start.4
  317.5 1.3 collective-permute-done.4
  318.8 3.6 collective-permute-start.5
  322.3 1.3 collective-permute-done.5
  323.6 3.6 collective-permute-start.6
  327.2 1.3 collective-permute-done.6
  328.5 0.8 select_reduce_fusion
  329.2 12.5 %all-reduce.2 = (f32[]{:T(128)}, f32[]{:T(128)}, f32[]{:T(128)}) all-reduce(f32[]{:T(128)} %get-tuple-element.7, f32[]{:T(128)} %get-tuple-element.8, f32[]{:T(128)} %get-tuple-element.6), channel_id=1, replica_groups=mesh['seq'=8,'vocab'=32] {'seq'}, use_global_device_ids=true, to_apply=%region_16.0 | all-reduce | flops 3 | bytes 24 | tf_op jit(solution)/shard_map/psum | solution.py:52
  343.7 0.6 select_divide_fusion
  344.3 2.5 multiply_convert_fusion
  346.8 1.0 copy-done.1
  347.9 14.2 %fusion = f32[2,128,5120]{1,2,0:T(8,128)} fusion(bf16[2,128,2432]{2,1,0:T(8,128)(2,1)S(1)} %multiply_convert_fusion, bf16[5120,2432]{1,0:T(8,128)(2,1)} %all-gather.2.cloned.1.call-done), kind=kOutput, calls=%fused_computation | convolution fusion | flops 6375342080 | bytes 31391744 | tf_op jit(solution)/shard_map/dot_general | solution.py:64
  362.1 222.7 %reduce-scatter.2.cloned.1.call-done = f32[2,128,160]{1,2,0:T(8,128)} async-done(((f32[2,128,5120]{1,2,0:T(8,128)}), f32[2,128,160]{1,2,0:T(8,128)}) %reduce-scatter.2.cloned.1.call-update) | async-done | bytes 163856 | tf_op jit(solution)/shard_map/reduce_scatter | solution.py:70
  584.7 1.6 convert_element_type.21
  (20 shorter events, 0.1 us)
Async XLA Ops:
  7.2 127.3 %copy-start = (bf16[2,128,5120]{2,1,0:T(8,128)(2,1)S(1)}, bf16[2,128,5120]{2,1,0:T(8,128)(2,1)}, u32[]{:S(2)}) copy-start(bf16[2,128,5120]{2,1,0:T(8,128)(2,1)} %param.7) | copy-start | bytes 7864324
  7.2 127.3 %all-gather.2.cloned.1.call-start = ((), (), s32[]{:S(2)}) async-start(), calls=%async_computation.1 | async-start | bytes 28016640 | tf_op jit(solution)/shard_map/all_gather | solution.py:18
  7.9 576.8 %reduce-scatter.2.cloned.1.call-start = ((), (), s32[]{:S(2)}) async-start(), calls=%async_computation.2 | async-start | bytes 5406720 | tf_op jit(solution)/shard_map/reduce_scatter | solution.py:70
  147.8 148.1 %copy-start.3 = (s32[2,128]{1,0:T(2,128)S(1)}, s32[2,128]{1,0:T(2,128)}, u32[]{:S(2)}) copy-start(s32[2,128]{1,0:T(2,128)} %param.12) | copy-start | bytes 3076
  147.8 148.1 %copy-start.4 = (f32[2]{0:T(128)S(1)}, f32[2]{0:T(128)}, u32[]{:S(2)}) copy-start(f32[2]{0:T(128)} %param.13) | copy-start | bytes 28
  147.8 148.1 %copy-start.5 = (s32[2]{0:T(128)S(1)}, s32[2]{0:T(128)}, u32[]{:S(2)}) copy-start(s32[2]{0:T(128)} %param.11) | copy-start | bytes 28
  147.8 196.5 %copy-start.2 = (s32[2,128]{1,0:T(2,128)S(1)}, s32[2,128]{1,0:T(2,128)}, u32[]{:S(2)}) copy-start(s32[2,128]{1,0:T(2,128)} %param.10) | copy-start | bytes 3076
  296.1 3.2 collective-permute-start
  299.4 4.8 collective-permute-start.1
  304.2 4.8 collective-permute-start.2
  309.1 4.8 collective-permute-start.3
  313.9 4.8 collective-permute-start.4
  318.8 4.8 collective-permute-start.5
  323.6 4.8 collective-permute-start.6
  346.8 1.0 copy-start.1
Sparse Core Ops, SparseCore 0:
  9.8 124.5 all-gather.1
  362.2 222.4 reduce-scatter.1
where the time goes:
time: 594 us; the launch traced here: 593 us
  waiting for transfers between devices  357 us (60%)
  blocking collectives  157 us (26%)
  matrix products  28.3 us (5%)
  starting transfers between devices  23.4 us (4%)
  between operations  16.2 us (3%)
  other arithmetic  9.68 us (2%)
    reduce_scatter x1, waiting for transfers between devices, per_device(): lax.psum_scatter(partial_grad, 'vocab', scatter_dimension=2, tiled=True)  223 us
    all_gather x1, waiting for transfers between devices, per_device(): whole_head = lax.all_gather(head_weight, 'seq', axis=0, tiled=True)  125 us
    pmax x1, blocking collectives, per_device(): top_policy, top_ref = lax.pmax((local_top, local_rtop), 'vocab')  75.2 us
    psum x1, blocking collectives, per_device(): lax.psum((jnp.sum(expo, axis=2), jnp.sum(jnp.exp(refs - top_ref[:, :, Non...  69.6 us
    ppermute x7, starting transfers between devices, from_behind(): return lax.ppermute(shard, axis, pairs)  23.3 us
    dot_general x1, matrix products, per_device(): lax.dot_general(logit_grad.reshape(batch * segment, vocab_dev), whole_hea...  14.2 us
    dot_general x1, matrix products, per_device(): jnp.dot(hidden.reshape(batch * segment, width), whole_head, preferred_ele...  13.4 us
    psum x1, blocking collectives, per_device(): lax.psum((jnp.sum(live), jnp.sum(live * returns), jnp.sum(live * returns...  12.5 us
  transfers between devices with their start and end apart: 9, of which 9 were waited for; matrix products, arithmetic and copies ran while one was open for 0% of the time, Pallas kernels for 0%

commit v1 on v0

--- a/solution.py
+++ b/solution.py
@@ -15,7 +15,8 @@
     vocab_dev = head_weight.shape[1]
     seq_start = lax.axis_index("seq") * segment
     vocab_start = lax.axis_index("vocab") * vocab_dev
-    whole_head = lax.all_gather(head_weight, "seq", axis=0, tiled=True)
+    stack = jnp.stack([head_weight] * lax.axis_size("seq"))
+    whole_head = jnp.concatenate(lax.all_to_all(stack, "seq", 0, 0), axis=0)
     logits = jnp.dot(
         hidden.reshape(batch * segment, width), whole_head, preferred_element_type=jnp.float32
     ).reshape(batch, segment, vocab_dev)

time: 594 us -> 760 us (1.28)
  waiting for transfers between devices: 357 us -> 499 us
  local copies, waits for them, and re-layouts: 1.05 us -> 15.8 us
  starting transfers between devices: 23.4 us -> 31.8 us
    all_to_all x0 -> x1, waiting for transfers between devices: none -> 269 us  [per_device(): whole_head = jnp.concatenate(lax.all_to_all(stack, 'seq', 0, 0), axis=0)]
    all_gather x1 -> x0, waiting for transfers between devices: 125 us -> none  [per_device(): whole_head = lax.all_gather(head_weight, 'seq', axis=0, tiled=True)]
    another operation x0 -> x1, local copies, waits for them, and re-layouts: none -> 14.7 us  [per_device(): stack = jnp.stack([head_weight] * lax.axis_size('seq'))]
    all_to_all x0 -> x1, starting transfers between devices: none -> 8.49 us  [per_device(): whole_head = jnp.concatenate(lax.all_to_all(stack, 'seq', 0, 0), axis=0)]
where the time goes in v1:
time: 760 us; the launch traced here: 759 us
  waiting for transfers between devices  499 us (66%)
  blocking collectives  158 us (21%)
  starting transfers between devices  31.8 us (4%)
  matrix products  28.3 us (4%)
  between operations  16.1 us (2%)
  local copies, waits for them, and re-layouts  15.8 us (2%)
  other arithmetic  9.68 us (1%)
    all_to_all x1, waiting for transfers between devices, per_device(): whole_head = jnp.concatenate(lax.all_to_all(stack, 'seq', 0, 0), axis=0)  269 us
    reduce_scatter x1, waiting for transfers between devices, per_device(): lax.psum_scatter(partial_grad, 'vocab', scatter_dimension=2, tiled=True)  221 us
    pmax x1, blocking collectives, per_device(): top_policy, top_ref = lax.pmax((local_top, local_rtop), 'vocab')  76.1 us
    psum x1, blocking collectives, per_device(): lax.psum((jnp.sum(expo, axis=2), jnp.sum(jnp.exp(refs - top_ref[:, :, Non...  69.6 us
    ppermute x7, starting transfers between devices, from_behind(): return lax.ppermute(shard, axis, pairs)  23.3 us
  transfers between devices with their start and end apart: 9, of which 9 were waited for; matrix products, arithmetic and copies ran while one was open for 0% of the time, Pallas kernels for 0%

profile of v1, /device:TPU:8, one launch (start us, length us, event | category | flops | bytes accessed | tf_op | source)
XLA Modules:
  0.0 758.7 jit_solution(6258219236786466544)
XLA Ops:
  7.2 14.7 %stack.2 = bf16[8,640,2432]{2,1,0:T(8,128)(2,1)} broadcast(bf16[640,2432]{1,0:T(8,128)(2,1)} %param.8), dimensions={1,2} | broadcast | bytes 28016640 | tf_op jit(solution)/shard_map/stack | solution.py:18
  21.9 8.5 %all-to-all-start = ((bf16[8,640,2432]{2,1,0:T(8,128)(2,1)}), bf16[8,640,2432]{2,1,0:T(8,128)(2,1)}, u32[]{:S(2)}, u32[]{:S(2)}) async-start(bf16[8,640,2432]{2,1,0:T(8,128)(2,1)} %stack.2), calls=%async_computation | async-start | bytes 49807360 | tf_op jit(solution)/shard_map/all_to_all | solution.py:19
  30.4 1.5 reduce_max.24
  31.9 268.7 %all-to-all-done = bf16[8,640,2432]{2,1,0:T(8,128)(2,1)} async-done(((bf16[8,640,2432]{2,1,0:T(8,128)(2,1)}), bf16[8,640,2432]{2,1,0:T(8,128)(2,1)}, u32[]{:S(2)}, u32[]{:S(2)}) %all-to-all-start) | async-done | bytes 24903712 | tf_op jit(solution)/shard_map/all_to_all | solution.py:19
  300.6 13.4 %fusion.10 = (f32[2,128]{1,0:T(2,128)S(1)}, f32[2,128,2432]{2,1,0:T(8,128)}) fusion(bf16[2,128,5120]{2,1,0:T(8,128)(2,1)S(1)} %copy-done, bf16[5120,2432,1]{1,0,2:T(8,128)(2,1)} %bitcast.1), kind=kOutput, calls=%fused_computation.24 | convolution fusion | flops 6375964672 | bytes 30016512 | tf_op jit(solution)/shard_map/dot_general | solution.py:20
  314.0 76.1 %all-reduce.1 = (f32[2,128]{1,0:T(2,128)S(1)}, f32[2,128]{1,0:T(2,128)S(1)}) all-reduce(f32[2,128]{1,0:T(2,128)S(1)} %get-tuple-element.23, bf16[2,128]{1,0:T(2,128)(2,1)S(1)} %reduce_max.24), channel_id=1, replica_groups=mesh['seq'=8,'vocab'=32] {'vocab'}, use_global_device_ids=true, to_apply=%region_1.0 | all-reduce | flops 512 | bytes 3584 | tf_op jit(solution)/shard_map/pmax | solution.py:26
  390.1 3.2 fusion.1
  393.3 69.6 %all-reduce = (f32[2,128]{1,0:T(2,128)S(1)}, f32[2,128]{1,0:T(2,128)S(1)}, f32[2,128]{1,0:T(2,128)S(1)}) all-reduce(f32[2,128]{1,0:T(2,128)S(1)} %get-tuple-element.4, f32[2,128]{1,0:T(2,128)S(1)} %get-tuple-element.5, f32[2,128]{1,0:T(2,128)S(1)} %get-tuple-element.3), channel_id=1, replica_groups=mesh['seq'=8,'vocab'=32] {'vocab'}, use_global_device_ids=true, to_apply=%region_5.0 | all-reduce | flops 768 | bytes 6144 | tf_op jit(solution)/shard_map/psum | solution.py:28
  463.0 0.2 fusion.8
  463.2 1.9 collective-permute-start
  465.1 1.3 collective-permute-done
  466.4 3.6 collective-permute-start.1
  469.9 1.3 collective-permute-done.1
  471.2 3.6 collective-permute-start.2
  474.8 1.3 collective-permute-done.2
  476.1 3.6 collective-permute-start.3
  479.6 1.3 collective-permute-done.3
  480.9 3.6 collective-permute-start.4
  484.5 1.3 collective-permute-done.4
  485.8 3.6 collective-permute-start.5
  489.3 1.3 collective-permute-done.5
  490.6 3.6 collective-permute-start.6
  494.2 1.3 collective-permute-done.6
  495.5 0.8 select_reduce_fusion
  496.2 12.5 %all-reduce.2 = (f32[]{:T(128)}, f32[]{:T(128)}, f32[]{:T(128)}) all-reduce(f32[]{:T(128)} %get-tuple-element.7, f32[]{:T(128)} %get-tuple-element.8, f32[]{:T(128)} %get-tuple-element.6), channel_id=1, replica_groups=mesh['seq'=8,'vocab'=32] {'seq'}, use_global_device_ids=true, to_apply=%region_16.0 | all-reduce | flops 3 | bytes 24 | tf_op jit(solution)/shard_map/psum | solution.py:53
  510.7 0.6 select_divide_fusion
  511.4 2.5 multiply_convert_fusion
  513.9 1.0 copy-done.1
  514.9 14.2 %fusion.11 = f32[2,128,5120]{1,2,0:T(8,128)} fusion(bf16[2,128,2432]{2,1,0:T(8,128)(2,1)S(1)} %multiply_convert_fusion, bf16[5120,2432,1]{1,0,2:T(8,128)(2,1)} %bitcast.1), kind=kOutput, calls=%fused_computation.25 | convolution fusion | flops 6375342080 | bytes 31391744 | tf_op jit(solution)/shard_map/dot_general | solution.py:65
  529.1 0.0 reduce-scatter.2.cloned.1.call-update
  529.1 221.2 %reduce-scatter.2.cloned.1.call-done = f32[2,128,160]{1,2,0:T(8,128)} async-done(((f32[2,128,5120]{1,2,0:T(8,128)}), f32[2,128,160]{1,2,0:T(8,128)}) %reduce-scatter.2.cloned.1.call-update) | async-done | bytes 163856 | tf_op jit(solution)/shard_map/reduce_scatter | solution.py:71
  750.3 1.6 convert_element_type.21
  (20 shorter events, 0.1 us)
Async XLA Ops:
  7.2 293.5 %copy-start = (bf16[2,128,5120]{2,1,0:T(8,128)(2,1)S(1)}, bf16[2,128,5120]{2,1,0:T(8,128)(2,1)}, u32[]{:S(2)}) copy-start(bf16[2,128,5120]{2,1,0:T(8,128)(2,1)} %param.7) | copy-start | bytes 7864324
  21.9 278.7 %all-to-all-start = ((bf16[8,640,2432]{2,1,0:T(8,128)(2,1)}), bf16[8,640,2432]{2,1,0:T(8,128)(2,1)}, u32[]{:S(2)}, u32[]{:S(2)}) async-start(bf16[8,640,2432]{2,1,0:T(8,128)(2,1)} %stack.2), calls=%async_computation | async-start | bytes 49807360 | tf_op jit(solution)/shard_map/all_to_all | solution.py:19
  30.4 719.9 %reduce-scatter.2.cloned.1.call-start = ((), (), s32[]{:S(2)}) async-start(), calls=%async_computation.2 | async-start | bytes 5406720 | tf_op jit(solution)/shard_map/reduce_scatter | solution.py:71
  314.0 149.0 %copy-start.3 = (s32[2,128]{1,0:T(2,128)S(1)}, s32[2,128]{1,0:T(2,128)}, u32[]{:S(2)}) copy-start(s32[2,128]{1,0:T(2,128)} %param.12) | copy-start | bytes 3076
  314.0 149.0 %copy-start.4 = (f32[2]{0:T(128)S(1)}, f32[2]{0:T(128)}, u32[]{:S(2)}) copy-start(f32[2]{0:T(128)} %param.13) | copy-start | bytes 28
  314.0 149.0 %copy-start.5 = (s32[2]{0:T(128)S(1)}, s32[2]{0:T(128)}, u32[]{:S(2)}) copy-start(s32[2]{0:T(128)} %param.11) | copy-start | bytes 28
  314.0 197.4 %copy-start.2 = (s32[2,128]{1,0:T(2,128)S(1)}, s32[2,128]{1,0:T(2,128)}, u32[]{:S(2)}) copy-start(s32[2,128]{1,0:T(2,128)} %param.10) | copy-start | bytes 3076
  463.2 3.2 collective-permute-start
  466.4 4.8 collective-permute-start.1
  471.2 4.8 collective-permute-start.2
  476.1 4.8 collective-permute-start.3
  480.9 4.8 collective-permute-start.4
  485.8 4.8 collective-permute-start.5
  490.6 4.8 collective-permute-start.6
  513.9 1.0 copy-start.1
Sparse Core Ops, SparseCore 0:
  529.2 221.0 reduce-scatter.1
